TPU v7x, 32 devices: a whole 2x2x4 slice. The times are simulated.
32 devices in a mesh: head: 8 (over z, y), dp: 4 (over x, core).
Axes of the slice: x: 2, y: 2, z: 4, core: 2. Of those that a mesh axis runs over, the one named last changes fastest.
Arguments:
- attn_out: bfloat16 [1024, 8192], P('dp', 'head'), may hold values from -6 to 6
- head_mask: int32 [64], P('head'), may hold values from 0 to 1, as said below
- gate_scale: float32 [64], P('head'), may hold values from 0.25 to 2
- w_out: bfloat16 [8192, 8192], P('head', 'dp'), may hold values from -0.09375 to 0.09375
- grad_out: bfloat16 [1024, 8192], P(('dp', 'head')), may hold values from -6 to 6
Outputs:
- proj_out: bfloat16 [1024, 8192], P(('dp', 'head'))
- grad_attn: bfloat16 [1024, 8192], P('dp', 'head')
- grad_w: float32 [8192, 8192], P('head', 'dp')
Inputs may be any that keep to these rules, and one draw needn't show every extreme that they name: `head_mask`: exactly 32 heads are live.
All inputs are finite; a program needn't handle non-finite values.
Results may differ from a plain program's by a relative error of at most 0.0051.
Values may be sent and summed in bfloat16 or wider, within the bound.
A program may use at most 128 MiB of HBM per device.

v0:
```python
import jax
import jax.numpy as jnp
from jax import lax
from jax.sharding import PartitionSpec as P


def shards(attn_out, head_mask, gate_scale, w_out, grad_out):
    gate_vals = head_mask.astype(jnp.float32) * gate_scale
    width_each = attn_out.shape[1] // gate_vals.shape[0]
    col_gate = jnp.repeat(gate_vals, width_each)
    gated = (attn_out.astype(jnp.float32) * col_gate[None, :]).astype(jnp.bfloat16)
    weight_rows = lax.all_gather(w_out, "dp", axis=1, tiled=True)
    proj_out = lax.psum_scatter(
        jnp.dot(gated, weight_rows, preferred_element_type=jnp.float32),
        "head",
        scatter_dimension=0,
        tiled=True,
    ).astype(jnp.bfloat16)
    grad_full = lax.all_gather(grad_out, "head", axis=0, tiled=True)
    back_proj = lax.dot_general(
        grad_full, weight_rows, (((1,), (1,)), ((), ())), preferred_element_type=jnp.float32
    )
    grad_attn = (back_proj * col_gate[None, :]).astype(jnp.bfloat16)
    grad_local = lax.dot_general(
        gated, grad_full, (((0,), (0,)), ((), ())), preferred_element_type=jnp.float32
    )
    grad_w = lax.psum_scatter(grad_local, "dp", scatter_dimension=1, tiled=True)
    return (proj_out, grad_attn, grad_w)


def solution(mesh):
    return jax.shard_map(
        shards,
        mesh=mesh,
        in_specs=(P("dp", "head"), P("head"), P("head"), P("head", "dp"), P(("dp", "head"), None)),
        out_specs=(P(("dp", "head"), None), P("dp", "head"), P("head", "dp")),
        check_vma=False,
    )
```

profile of v0, /device:TPU:0, one launch (start us, length us, event | category | flops | bytes accessed | tf_op | source)
XLA Modules:
  0.0 583.7 jit_solution(12137804477661444461)
XLA Ops:
  7.2 0.0 all-gather.3.cloned.1.call-start
  7.2 0.7 all-gather.3.cloned.1.call-update
  7.9 0.0 all-gather.5.cloned.1.call-start
  7.9 0.7 all-gather.5.cloned.1.call-update
  8.6 0.0 reduce-scatter.3.cloned.1.call-start
  8.7 0.7 convert_multiply_fusion
  9.4 0.1 broadcast_bitcast_fusion
  9.4 108.7 %all-gather.3.cloned.1.call-done = bf16[1024,8192]{1,0:T(8,128)(2,1)} async-done(((bf16[1024,2048]{1,0:T(8,128)(2,1)}), bf16[1024,8192]{1,0:T(8,128)(2,1)}) %all-gather.3.cloned.1.call-update) | async-done | bytes 16777232 | tf_op jit(solution)/shard_map/all_gather | solution.py:12
  118.2 13.7 %fusion.2 = f32[256,8192]{1,0:T(8,128)} fusion(bf16[1024,8192]{1,0:T(8,128)(2,1)} %all-gather.3.cloned.1.call-done, bf16[256,1024]{1,0:T(8,128)(2,1)} %param.5, f32[1024]{0:T(1024)S(1)} %broadcast_bitcast_fusion), kind=kOutput, calls=%fused_computation.4 | convolution fusion | flops 4295753728 | bytes 25694208 | tf_op jit(solution)/shard_map/dot_general | solution.py:14
  131.9 0.0 copy-start
  131.9 0.0 reduce-scatter.3.cloned.1.call-update
  131.9 0.0 reduce-scatter.5.cloned.1.call-start
  131.9 61.2 %all-gather.5.cloned.1.call-done = bf16[256,8192]{1,0:T(8,128)(2,1)} async-done(((bf16[32,8192]{1,0:T(8,128)(2,1)}), bf16[256,8192]{1,0:T(8,128)(2,1)}) %all-gather.5.cloned.1.call-update) | async-done | bytes 4194320 | tf_op jit(solution)/shard_map/all_gather | solution.py:19
  193.1 0.0 copy-done
  193.1 15.9 %fusion.1 = f32[1024,8192]{1,0:T(8,128)} fusion(bf16[256,8192]{1,0:T(8,128)(2,1)} %all-gather.5.cloned.1.call-done, bf16[256,1024]{1,0:T(8,128)(2,1)S(1)} %copy-done, f32[1024]{0:T(1024)S(1)} %broadcast_bitcast_fusion), kind=kOutput, calls=%fused_computation.3 | convolution fusion | flops 4295753728 | bytes 38277120 | tf_op jit(solution)/shard_map/dot_general | solution.py:24
  209.0 0.0 reduce-scatter.5.cloned.1.call-update
  209.1 12.5 %fusion = bf16[256,1024]{1,0:T(8,128)(2,1)} fusion(bf16[256,8192]{1,0:T(8,128)(2,1)} %all-gather.5.cloned.1.call-done, bf16[1024,8192]{1,0:T(8,128)(2,1)} %all-gather.3.cloned.1.call-done, f32[1024]{0:T(1024)S(1)} %broadcast_bitcast_fusion), kind=kOutput, calls=%fused_computation.1 | convolution fusion | flops 4295491584 | bytes 21499904 | tf_op jit(solution)/shard_map/dot_general | solution.py:20
  221.5 121.3 %reduce-scatter.3.cloned.1.call-done = f32[32,8192]{1,0:T(8,128)} async-done(((f32[256,8192]{1,0:T(8,128)}), f32[32,8192]{1,0:T(8,128)}) %reduce-scatter.3.cloned.1.call-update) | async-done | bytes 1048592 | tf_op jit(solution)/shard_map/reduce_scatter | solution.py:13
  342.8 2.1 convert_element_type.18
  344.9 232.3 %reduce-scatter.5.cloned.1.call-done = f32[1024,2048]{1,0:T(8,128)} async-done(((f32[1024,8192]{1,0:T(8,128)}), f32[1024,2048]{1,0:T(8,128)}) %reduce-scatter.5.cloned.1.call-update) | async-done | bytes 8388624 | tf_op jit(solution)/shard_map/reduce_scatter | solution.py:27
Async XLA Ops:
  7.2 111.0 %all-gather.3.cloned.1.call-start = ((), (), s32[]{:S(2)}) async-start(), calls=%async_computation.2 | async-start | bytes 20971520 | tf_op jit(solution)/shard_map/all_gather | solution.py:12
  7.9 185.2 %all-gather.5.cloned.1.call-start = ((), (), s32[]{:S(2)}) async-start(), calls=%async_computation.4 | async-start | bytes 4718592 | tf_op jit(solution)/shard_map/all_gather | solution.py:19
  8.6 334.2 %reduce-scatter.3.cloned.1.call-start = ((), (), s32[]{:S(2)}) async-start(), calls=%async_computation.3 | async-start | bytes 9437184 | tf_op jit(solution)/shard_map/reduce_scatter | solution.py:13
  131.9 61.3 %copy-start = (bf16[256,1024]{1,0:T(8,128)(2,1)S(1)}, bf16[256,1024]{1,0:T(8,128)(2,1)}, u32[]{:S(2)}) copy-start(bf16[256,1024]{1,0:T(8,128)(2,1)} %param.5) | copy-start | bytes 1572868
  131.9 445.3 %reduce-scatter.5.cloned.1.call-start = ((), (), s32[]{:S(2)}) async-start(), calls=%async_computation.5 | async-start | bytes 41943040 | tf_op jit(solution)/shard_map/reduce_scatter | solution.py:27
Sparse Core Ops, SparseCore 0:
  9.5 108.6 all-gather.2
  120.3 72.7 all-gather.4
  196.8 145.9 reduce-scatter.2
  345.8 231.3 reduce-scatter.4
where the time goes:
time: 584 us
  waiting for transfers between devices  525 us (90%)
  matrix products  42.1 us (7%)
  between operations  13.8 us (2%)
    reduce_scatter x1, waiting for transfers between devices, shards(): grad_w = lax.psum_scatter(grad_local, 'dp', scatter_dimension=1, tiled=True)  232 us
    reduce_scatter x1, waiting for transfers between devices, shards(): lax.psum_scatter(jnp.dot(gated, weight_rows, preferred_element_type=jnp.f...  121 us
    all_gather x1, waiting for transfers between devices, shards(): weight_rows = lax.all_gather(w_out, 'dp', axis=1, tiled=True)  109 us
    all_gather x1, waiting for transfers between devices, shards(): grad_full = lax.all_gather(grad_out, 'head', axis=0, tiled=True)  61.2 us
    dot_general x1, matrix products, shards(): lax.dot_general(gated, grad_full, (((0,), (0,)), ((), ())), preferred_ele...  15.9 us
    dot_general x1, matrix products, shards(): jnp.dot(gated, weight_rows, preferred_element_type=jnp.float32)  13.7 us
    dot_general x1, matrix products, shards(): lax.dot_general(grad_full, weight_rows, (((1,), (1,)), ((), ())), preferr...  12.5 us
  transfers between devices with their start and end apart: 4, of which 4 were waited for; matrix products, arithmetic and copies ran while one was open for 8% of the time, Pallas kernels for 0%

commit v1 on v0

--- a/solution.py
+++ b/solution.py
@@ -9,7 +9,7 @@
     width_each = attn_out.shape[1] // gate_vals.shape[0]
     col_gate = jnp.repeat(gate_vals, width_each)
     gated = (attn_out.astype(jnp.float32) * col_gate[None, :]).astype(jnp.bfloat16)
-    weight_rows = lax.all_gather(w_out, "dp", axis=1, tiled=True)
+    weight_rows = jnp.concatenate(lax.all_gather(w_out, "dp"), axis=1)
     proj_out = lax.psum_scatter(
         jnp.dot(gated, weight_rows, preferred_element_type=jnp.float32),
         "head",

time: 584 us -> 584 us (level)
  waiting for transfers between devices: 525 us -> 497 us
  local copies, waits for them, and re-layouts: 0.08 us -> 22.7 us
    all_gather x1, waiting for transfers between devices: 61.2 us -> 33.1 us  [shards(): grad_full = lax.all_gather(grad_out, 'head', axis=0, tiled=True)]
    reshape x0 -> x1, local copies, waits for them, and re-layouts: none -> 22.7 us  [shards(): weight_rows = jnp.concatenate(lax.all_gather(w_out, 'dp'), axis=1)]
  transfers between devices with their start and end apart: 4 -> 4, of which waited for: 4 -> 4; matrix products, arithmetic and copies ran while one was open for 8% -> 12% of each run, Pallas kernels for 0% -> 0%
where the time goes in v1:
time: 584 us
  waiting for transfers between devices  497 us (85%)
  matrix products  47.5 us (8%)
  local copies, waits for them, and re-layouts  22.7 us (4%)
  between operations  13.8 us (2%)
    reduce_scatter x1, waiting for transfers between devices, shards(): grad_w = lax.psum_scatter(grad_local, 'dp', scatter_dimension=1, tiled=True)  232 us
    reduce_scatter x1, waiting for transfers between devices, shards(): lax.psum_scatter(jnp.dot(gated, weight_rows, preferred_element_type=jnp.f...  121 us
    all_gather x1, waiting for transfers between devices, shards(): weight_rows = jnp.concatenate(lax.all_gather(w_out, 'dp'), axis=1)  109 us
    all_gather x1, waiting for transfers between devices, shards(): grad_full = lax.all_gather(grad_out, 'head', axis=0, tiled=True)  33.1 us
    reshape x1, local copies, waits for them, and re-layouts, shards(): weight_rows = jnp.concatenate(lax.all_gather(w_out, 'dp'), axis=1)  22.7 us
    dot_general x1, matrix products, shards(): jnp.dot(gated, weight_rows, preferred_element_type=jnp.float32)  19.1 us
    dot_general x1, matrix products, shards(): lax.dot_general(gated, grad_full, (((0,), (0,)), ((), ())), preferred_ele...  15.9 us
    dot_general x1, matrix products, shards(): lax.dot_general(grad_full, weight_rows, (((1,), (1,)), ((), ())), preferr...  12.4 us
  transfers between devices with their start and end apart: 4, of which 4 were waited for; matrix products, arithmetic and copies ran while one was open for 12% of the time, Pallas kernels for 0%

profile of v1, /device:TPU:0, one launch (start us, length us, event | category | flops | bytes accessed | tf_op | source)
XLA Modules:
  0.0 583.7 jit_solution(817551873693366502)
XLA Ops:
  7.2 0.0 all-gather.6.cloned.1.call-start
  7.2 0.7 all-gather.6.cloned.1.call-update
  7.9 0.0 all-gather.4.cloned.1.call-start
  7.9 0.7 all-gather.4.cloned.1.call-update
  8.6 0.0 reduce-scatter.3.cloned.1.call-start
  8.7 0.7 convert_multiply_fusion
  9.4 0.1 broadcast_bitcast_fusion
  9.4 108.7 %all-gather.6.cloned.1.call-done = bf16[4096,2048]{1,0:T(8,128)(2,1)} async-done(((bf16[1024,2048]{1,0:T(8,128)(2,1)}), bf16[4096,2048]{1,0:T(8,128)(2,1)}) %all-gather.6.cloned.1.call-update) | async-done | bytes 16777232 | tf_op jit(solution)/shard_map/all_gather | solution.py:12
  118.2 0.0 copy-start
  118.2 22.7 %copy.8 = bf16[1024,4,2048]{0,2,1:T(8,128)(2,1)} copy(bf16[1024,4,2048]{2,0,1:T(8,128)(2,1)} %bitcast.12) | data formatting | bytes 33554432 | tf_op jit(solution)/shard_map/reshape | solution.py:12
  140.8 0.0 copy-done
  140.8 19.1 %fusion.2 = f32[256,8192]{1,0:T(8,128)} fusion(bf16[1024,8192]{0,1:T(8,128)(2,1)} %bitcast.10, bf16[256,1024]{1,0:T(8,128)(2,1)S(1)} %copy-done, f32[1024]{0:T(1024)S(1)} %broadcast_bitcast_fusion), kind=kOutput, calls=%fused_computation.4 | convolution fusion | flops 4295753728 | bytes 25694208 | tf_op jit(solution)/shard_map/dot_general | solution.py:14
  160.0 0.0 reduce-scatter.3.cloned.1.call-update
  160.0 0.0 reduce-scatter.5.cloned.1.call-start
  160.0 33.1 %all-gather.4.cloned.1.call-done = bf16[256,8192]{1,0:T(8,128)(2,1)} async-done(((bf16[32,8192]{1,0:T(8,128)(2,1)}), bf16[256,8192]{1,0:T(8,128)(2,1)}) %all-gather.4.cloned.1.call-update) | async-done | bytes 4194320 | tf_op jit(solution)/shard_map/all_gather | solution.py:19
  193.2 15.9 %fusion.1 = f32[1024,8192]{1,0:T(8,128)} fusion(bf16[256,8192]{1,0:T(8,128)(2,1)} %all-gather.4.cloned.1.call-done, bf16[256,1024]{1,0:T(8,128)(2,1)S(1)} %copy-done, f32[1024]{0:T(1024)S(1)} %broadcast_bitcast_fusion), kind=kOutput, calls=%fused_computation.3 | convolution fusion | flops 4295753728 | bytes 38277120 | tf_op jit(solution)/shard_map/dot_general | solution.py:24
  209.1 0.0 reduce-scatter.5.cloned.1.call-update
  209.1 12.4 %fusion = bf16[256,1024]{1,0:T(8,128)(2,1)} fusion(bf16[256,8192]{1,0:T(8,128)(2,1)} %all-gather.4.cloned.1.call-done, bf16[1024,8192]{0,1:T(8,128)(2,1)} %bitcast.11, f32[1024]{0:T(1024)S(1)} %broadcast_bitcast_fusion), kind=kOutput, calls=%fused_computation.1 | convolution fusion | flops 4295491584 | bytes 21499904 | tf_op jit(solution)/shard_map/dot_general | solution.py:20
  221.5 121.2 %reduce-scatter.3.cloned.1.call-done = f32[32,8192]{1,0:T(8,128)} async-done(((f32[256,8192]{1,0:T(8,128)}), f32[32,8192]{1,0:T(8,128)}) %reduce-scatter.3.cloned.1.call-update) | async-done | bytes 1048592 | tf_op jit(solution)/shard_map/reduce_scatter | solution.py:13
  342.8 2.1 convert_element_type.18
  344.8 232.3 %reduce-scatter.5.cloned.1.call-done = f32[1024,2048]{1,0:T(8,128)} async-done(((f32[1024,8192]{1,0:T(8,128)}), f32[1024,2048]{1,0:T(8,128)}) %reduce-scatter.5.cloned.1.call-update) | async-done | bytes 8388624 | tf_op jit(solution)/shard_map/reduce_scatter | solution.py:27
Async XLA Ops:
  7.2 111.0 %all-gather.6.cloned.1.call-start = ((), (), s32[]{:S(2)}) async-start(), calls=%async_computation.5 | async-start | bytes 20971520 | tf_op jit(solution)/shard_map/all_gather | solution.py:12
  7.9 185.3 %all-gather.4.cloned.1.call-start = ((), (), s32[]{:S(2)}) async-start(), calls=%async_computation.3 | async-start | bytes 4718592 | tf_op jit(solution)/shard_map/all_gather | solution.py:19
  8.6 334.1 %reduce-scatter.3.cloned.1.call-start = ((), (), s32[]{:S(2)}) async-start(), calls=%async_computation.2 | async-start | bytes 9437184 | tf_op jit(solution)/shard_map/reduce_scatter | solution.py:13
  118.2 22.7 %copy-start = (bf16[256,1024]{1,0:T(8,128)(2,1)S(1)}, bf16[256,1024]{1,0:T(8,128)(2,1)}, u32[]{:S(2)}) copy-start(bf16[256,1024]{1,0:T(8,128)(2,1)} %param.5) | copy-start | bytes 1572868
  160.0 417.2 %reduce-scatter.5.cloned.1.call-start = ((), (), s32[]{:S(2)}) async-start(), calls=%async_computation.4 | async-start | bytes 41943040 | tf_op jit(solution)/shard_map/reduce_scatter | solution.py:27
Sparse Core Ops, SparseCore 0:
  9.5 108.6 all-gather.5
  120.3 72.8 all-gather.3
  196.8 145.9 reduce-scatter.2
  345.8 231.3 reduce-scatter.4
